TPU v7x, 256 devices: a whole 4x4x8 slice. The times are simulated.
256 devices in a mesh: mod: 16 (over z, y_lo), pulse: 16 (over y_hi, x, core).
Axes of the slice: x: 4, y: 4 (y_hi: 2, y_lo: 2; y = y_hi * 2 + y_lo), z: 8, core: 2. Of those that a mesh axis runs over, the one named last changes fastest.
Arguments:
- raw_frames: bfloat16 [16, 16, 16, 128, 512], P('pulse', None, 'mod'), may hold values from -6 to 6
- gain_section: int32 [16, 16, 16, 16, 512], P('pulse', None, 'mod'), may hold values from 0 to 6560, as said below
- offset: float32 [16, 3, 128, 512], P('mod'), may hold values from -3 to 3
- gain_factor: float32 [16, 3, 128, 512], P('mod'), may hold values from 0.5 to 2
- row_map: bfloat16 [1024, 1024], replicated, as said below
- column_map: bfloat16 [1024, 1024], replicated
- reference_image: bfloat16 [1024, 1024], P(('mod', 'pulse')), may hold values from -6 to 6
- shifts: int32 [2, 16, 16, 64], P(None, 'pulse', 'mod'), may hold values from -24 to 24
Outputs:
- scores: float32 [16, 16, 64], P('pulse', 'mod')
- new_reference: float32 [1024, 1024], P(('mod', 'pulse'))
Inputs may be any that keep to these rules, and one draw needn't show every extreme that they name: `gain_section`: each word holds the gain sections 0, 1 or 2 of 8 consecutive pixel rows in base 3, row 8 p + k as the digit of 3 ** k. row_map and column_map are the identity plus a dense interpolation part.
All inputs are finite; a program needn't handle non-finite values.
Results may differ from a plain program's by a relative error of at most 0.0005.
The roundings to bfloat16 on the way count: a program that leaves them out, or rounds other values in their place, can miss the bound.
Values may be sent and summed in bfloat16 or wider, within the bound.
A program may use at most 128 MiB of HBM per device.

v0:
```python
import jax
import jax.numpy as jnp
from jax import lax
from jax.sharding import PartitionSpec as P

MR = 128
MC = 512
TS = 128
SH = 24
TILES = 64
prior_weight = 16.0


def unpack_section(packed):
    powers = jnp.array([1, 3, 9, 27, 81, 243, 729, 2187], dtype=jnp.int32)
    section = jnp.remainder(jnp.floor_divide(packed[..., :, None, :], powers[:, None]), 3)
    return section.reshape(packed.shape[:-2] + (packed.shape[-2] * 8, packed.shape[-1]))


def calibrate(raw_frames, gain_section, offset, gain_factor):
    dark_level = jnp.where(
        gain_section == 0, offset[:, 0], jnp.where(gain_section == 1, offset[:, 1], offset[:, 2])
    )
    factor = jnp.where(
        gain_section == 0,
        gain_factor[:, 0],
        jnp.where(gain_section == 1, gain_factor[:, 1], gain_factor[:, 2]),
    )
    return ((raw_frames.astype(jnp.float32) - dark_level) * factor).astype(jnp.bfloat16)


def assemble(modules_now):
    quadrants = modules_now.reshape(2, 2, 4, MR, MC)
    return quadrants.transpose(0, 2, 3, 1, 4).reshape(8 * MR, 2 * MC)


def frame_image(modules_now, row_map, column_map):
    assembled = assemble(modules_now)
    row_mapped = jnp.dot(row_map, assembled, preferred_element_type=jnp.float32).astype(
        jnp.bfloat16
    )
    return jnp.dot(row_mapped, column_map, preferred_element_type=jnp.float32).astype(jnp.bfloat16)


def track_tiles(lab_image, ref_padded, shift_rows, shift_cols, splat_map, cover_map):
    tiles_across = lab_image.shape[1] // TS
    tiles_count = lab_image.shape[0] // TS * tiles_across

    def tile_step(index, carried):
        splat_map, cover_map, scores = carried
        index = jnp.asarray(index).astype(jnp.int32)
        row_start = index // tiles_across * TS
        col_start = index % tiles_across * TS
        top_edge = row_start + shift_rows[index] + SH
        left_edge = col_start + shift_cols[index] + SH
        frame_tile = lax.dynamic_slice(lab_image, (row_start, col_start), (TS, TS)).astype(
            jnp.float32
        )
        window = lax.dynamic_slice(ref_padded, (top_edge, left_edge), (TS, TS)).astype(jnp.float32)
        score_value = jnp.sum(frame_tile * window) / TS
        weight = jax.nn.sigmoid(score_value)
        current = lax.dynamic_slice(splat_map, (top_edge, left_edge), (TS, TS))
        splat_map = lax.dynamic_update_slice(
            splat_map, current + weight * frame_tile, (top_edge, left_edge)
        )
        scores = scores.at[index].set(score_value)
        return (splat_map, cover_map, scores)

    start = (splat_map, cover_map, jnp.zeros((tiles_count,), jnp.float32))
    return lax.fori_loop(0, tiles_count, tile_step, start)


def reduce_single(splat_map):
    return lax.psum_scatter(splat_map, ("mod", "pulse"), scatter_dimension=0, tiled=True)


def recount(scores, shift_rows, shift_cols, height, width):
    weights = jax.nn.sigmoid(scores)
    all_weights, all_rows, all_cols = (
        lax.all_gather(weights, ("mod", "pulse"), axis=0, tiled=True),
        lax.all_gather(shift_rows.astype(jnp.float32), ("mod", "pulse"), axis=0, tiled=True),
        lax.all_gather(shift_cols.astype(jnp.float32), ("mod", "pulse"), axis=0, tiled=True),
    )
    tiles_across = width // TS
    tile_index = jnp.arange(TILES)
    base_rows = (tile_index // tiles_across * TS).astype(jnp.float32)
    base_cols = (tile_index % tiles_across * TS).astype(jnp.float32)
    group_size = 32
    block_count = all_weights.shape[0] // group_size
    block_width = group_size * TILES
    weight_blocks = all_weights.reshape(block_count, block_width)
    top_blocks = (all_rows + base_rows[None, :]).reshape(block_count, block_width)
    left_blocks = (all_cols + base_cols[None, :]).reshape(block_count, block_width)
    row_count = height // (lax.axis_size("mod") * lax.axis_size("pulse"))
    owner_index = lax.axis_index("mod") * lax.axis_size("pulse") + lax.axis_index("pulse")
    owner_rows = (owner_index * row_count + jnp.arange(row_count)).astype(jnp.float32)
    all_columns = jnp.arange(width).astype(jnp.float32)

    def add_block(running, block):
        weight_now, top_now, left_now = block
        row_hit = (
            (owner_rows[:, None] >= top_now[None, :])
            & (owner_rows[:, None] < top_now[None, :] + TS)
        ).astype(jnp.float32)
        col_hit = (
            (all_columns[None, :] >= left_now[:, None])
            & (all_columns[None, :] < left_now[:, None] + TS)
        ).astype(jnp.float32)
        product = jnp.dot(
            row_hit * weight_now[None, :],
            col_hit,
            precision=lax.Precision.HIGHEST,
            preferred_element_type=jnp.float32,
        )
        return (running + product, None)

    empty = jnp.zeros((row_count, width), jnp.float32)
    return lax.scan(add_block, empty, (weight_blocks, top_blocks, left_blocks))[0]


def per_device(
    raw_frames, gain_section, offset, gain_factor, row_map, column_map, reference_image, shifts
):
    calibrated = calibrate(raw_frames, unpack_section(gain_section), offset, gain_factor)
    regrouped = lax.all_to_all(calibrated, "mod", split_axis=1, concat_axis=2, tiled=True)
    whole_reference = lax.all_gather(reference_image, ("mod", "pulse"), axis=0, tiled=True)
    height = 8 * MR
    width = 2 * MC
    ref_padded = jnp.pad(whole_reference, SH)
    empty = jnp.zeros((height + 2 * SH, width + 2 * SH), jnp.float32)
    frames = regrouped[0]
    shift_rows = shifts[0, 0]
    shift_cols = shifts[1, 0]

    def per_frame(carried, inputs):
        modules_now, rows_now, cols_now = inputs
        lab_image = frame_image(modules_now, row_map, column_map)
        splat_map, cover_map, scores = track_tiles(
            lab_image, ref_padded, rows_now, cols_now, carried[0], carried[1]
        )
        return ((splat_map, cover_map), scores)

    (splat_map, cover_map), scores = lax.scan(
        per_frame, (empty, empty), (frames, shift_rows, shift_cols)
    )
    splat_map = splat_map[SH : SH + height, SH : SH + width]
    owned_splat = reduce_single(splat_map)
    owned_cover = recount(scores, shift_rows, shift_cols, height, width)
    new_reference = (owned_splat + prior_weight * reference_image.astype(jnp.float32)) / (
        owned_cover + prior_weight
    )
    return (scores.reshape(1, scores.shape[0], scores.shape[1]), new_reference)


def solution(mesh):
    return jax.shard_map(
        per_device,
        mesh=mesh,
        in_specs=(
            P("pulse", None, "mod", None, None),
            P("pulse", None, "mod", None, None),
            P("mod", None, None, None),
            P("mod", None, None, None),
            P(),
            P(),
            P(("mod", "pulse"), None),
            P(None, "pulse", "mod", None),
        ),
        out_specs=(P("pulse", "mod", None), P(("mod", "pulse"), None)),
        check_vma=False,
    )
```

profile of v0, /device:TPU:1, one launch (start us, length us, event | category | flops | bytes accessed | tf_op | source)
XLA Modules:
  0.0 1815.0 jit_solution(10373691381890550767)
XLA Ops:
  11.3 46.8 %multiply_convert_fusion = bf16[1,16,1,128,512]{4,3,2,0,1:T(8,128)(2,1)} fusion(bf16[1,16,1,128,512]{4,3,2,1,0:T(8,128)(2,1)S(1)} %copy-done.1, f32[128,512]{1,0:T(8,128)S(1)} %get-tuple-element.391, f32[128,512]{1,0:T(8,128)S(1)} %get-tuple-element.392, f32[128,512]{1,0:T(8,128)S(1)} %get-tuple-element.390, f32[128,512]{1,0:T(8,128)S(1)} %get-tuple-element.398, ...), kind=kLoop, calls=%fused_computation.36 | loop fusion | flops 23068672 | bytes 6423040 | tf_op jit(solution)/shard_map/convert_element_type | solution.py:29
  58.1 10.2 all-to-all-start
  69.3 47.6 %all-to-all-done = bf16[1,16,1,128,512]{4,3,2,0,1:T(8,128)(2,1)} async-done(((bf16[1,16,1,128,512]{4,3,2,0,1:T(8,128)(2,1)}), bf16[1,16,1,128,512]{4,3,2,0,1:T(8,128)(2,1)}, u32[]{:S(2)}, u32[]{:S(2)}) %all-to-all-start) | async-done | bytes 2097184 | tf_op jit(solution)/shard_map/all_to_all | solution.py:125
  117.0 3.8 copy.13
  122.6 8.2 fusion.26
  130.8 360.6 %all-gather.6.cloned.1.call-done = bf16[256,4,1024]{2,1,0:T(4,128)(2,1)} async-done(((bf16[1,4,1024]{2,1,0:T(4,128)(2,1)}), bf16[256,4,1024]{2,1,0:T(4,128)(2,1)}) %all-gather.6.cloned.1.call-update) | async-done | bytes 2097168 | tf_op jit(solution)/shard_map/all_gather | solution.py:126
  491.5 4.0 reshape.340
  495.4 4.2 pad.8
  502.2 589.1 %while.40 = (s32[]{:T(128)}, f32[1072,1072]{1,0:T(8,128)}, f32[64]{0:T(128)S(1)}, s32[64]{0:T(128)S(1)}, s32[64]{0:T(128)S(1)}, /*index=5*/bf16[1024,1024]{1,0:T...) while((s32[]{:T(128)}, f32[1072,1072]{1,0:T(8,128)}, ...), condition=%wide.region_2.3_spmd, body=%wide.region_0.2_spmd.sunk | while | flops 114727 | bytes 361614 | solution.py:70
  508.0 3.3 dynamic_update_slice.15
  526.5 3.3 dynamic_update_slice.15
  609.3 3.2 dynamic_update_slice.15
  627.8 3.3 dynamic_update_slice.15
  673.9 3.3 dynamic_update_slice.15
  692.4 3.2 dynamic_update_slice.15
  710.9 3.2 dynamic_update_slice.15
  766.2 3.3 dynamic_update_slice.15
  775.4 3.3 dynamic_update_slice.15
  793.9 3.3 dynamic_update_slice.15
  812.4 3.2 dynamic_update_slice.15
  830.8 3.2 dynamic_update_slice.15
  840.0 3.2 dynamic_update_slice.15
  849.3 3.3 dynamic_update_slice.15
  877.0 3.2 dynamic_update_slice.15
  895.4 3.3 dynamic_update_slice.15
  913.9 3.3 dynamic_update_slice.15
  941.6 3.2 dynamic_update_slice.15
  1015.4 3.3 dynamic_update_slice.15
  1091.3 5.5 slice.52
  1097.6 343.4 %all-gather = f32[256,1,1,64]{3,2,1,0:T(1,128)S(1)} all-gather(f32[1,1,1,64]{3,2,1,0:T(1,128)S(1)} %get-tuple-element.394), channel_id=2, replica_groups=mesh['mod'=16,'pulse'=16] {'mod','pulse'}, dimensions={0}, use_global_device_ids=true | all-gather | bytes 65792 | tf_op jit(solution)/shard_map/all_gather | solution.py:81
  1441.2 339.5 %all-gather.2 = f32[256,1,1,64]{3,2,1,0:T(1,128)S(1)} all-gather(f32[1,1,1,64]{3,2,1,0:T(1,128)S(1)} %get-tuple-element.393), channel_id=4, replica_groups=mesh['mod'=16,'pulse'=16] {'mod','pulse'}, dimensions={0}, use_global_device_ids=true | all-gather | bytes 65792 | tf_op jit(solution)/shard_map/all_gather | solution.py:82
  1781.7 25.1 %while.41 = (s32[]{:T(128)}, f32[4,1024]{1,0:T(4,128)S(1)}, f32[8,2048]{1,0:T(8,128)S(1)}, f32[8,2048]{1,0:T(8,128)S(1)}, f32[8,2048]{1,0:T(8,128)S(1)}, /*index=5*/s32[]{:T(128)}, s32[]{:T(128)}, s32[]{:T(128)}) while((s32[]{:T(128)}, f32[4,1024]{1,0:T(4,128)S(1)}, f32[8,2048]{1,0:T(8,128)S(1)}, ...), condition=%wide.region_5.6_spmd.clone.clone, body=%wide.region_4.5_spmd.clone.clone.sunk | while | flops 107000840 | bytes 155787 | solution.py:118
  (449 shorter events, 433.5 us)
Async XLA Ops:
  7.2 115.4 %copy-start = (bf16[1024,1024]{1,0:T(8,128)(2,1)S(1)}, bf16[1024,1024]{1,0:T(8,128)(2,1)}, u32[]{:S(2)}) copy-start(bf16[1024,1024]{1,0:T(8,128)(2,1)} %param.20) | copy-start | bytes 6291460
  9.3 2.1 copy-start.1
  11.3 58.0 %copy-start.5 = (s32[2,1,1,64]{3,2,1,0:T(1,128)S(1)}, s32[2,1,1,64]{3,2,1,0:T(1,128)}, u32[]{:S(2)}) copy-start(s32[2,1,1,64]{3,2,1,0:T(1,128)} %param.22) | copy-start | bytes 1540
  58.1 58.8 %all-to-all-start = ((bf16[1,16,1,128,512]{4,3,2,0,1:T(8,128)(2,1)}), bf16[1,16,1,128,512]{4,3,2,0,1:T(8,128)(2,1)}, u32[]{:S(2)}, u32[]{:S(2)}) async-start(bf16[1,16,1,128,512]{4,3,2,0,1:T(8,128)(2,1)} %multiply_convert_fusion), calls=%async_computation | async-start | bytes 4194304 | tf_op jit(solution)/shard_map/all_to_all | solution.py:125
  68.3 423.1 %all-gather.6.cloned.1.call-start = ((), (), s32[]{:S(2)}) async-start(), calls=%async_computation.1 | async-start | bytes 2105344 | tf_op jit(solution)/shard_map/all_gather | solution.py:126
  69.1 1711.7 %all-reduce.6.cloned.1.call-start = ((), (), s32[]{:S(2)}) async-start(), calls=%async_computation.2 | async-start | bytes 8519680
  1091.3 5.5 copy-start.4
  1096.9 0.6 copy-start.2
  1781.7 25.2 %copy-start.3 = (bf16[4,1024]{1,0:T(4,128)(2,1)S(1)}, bf16[4,1024]{1,0:T(4,128)(2,1)}, u32[]{:S(2)}) copy-start(bf16[4,1024]{1,0:T(4,128)(2,1)} %param.21) | copy-start | bytes 24580
Sparse Core Ops, SparseCore 0:
  71.0 420.3 all-gather.5
  1097.7 271.1 all-reduce.5
where the time goes:
time: 1830 us; the launch traced here: 1820 us
  blocking collectives  683 us (37%)
  waiting for transfers between devices  409 us (22%)
  local copies, waits for them, and re-layouts  307 us (17%)
  other arithmetic  227 us (12%)
  loops' own time  132 us (7%)
  matrix products  32.6 us (2%)
    all_gather x1, waiting for transfers between devices, per_device(): lax.all_gather(reference_image, ('mod', 'pulse'), axis=0, tiled=True)  361 us
    all_gather x1, blocking collectives, recount(): lax.all_gather(shift_rows.astype(jnp.float32), ('mod', 'pulse'), axis=0,...  343 us
    all_gather x1, blocking collectives, recount(): lax.all_gather(shift_cols.astype(jnp.float32), ('mod', 'pulse'), axis=0,...  339 us
    dynamic_update_slice x64, local copies, waits for them, and re-layouts, tile_step(): lax.dynamic_update_slice(splat_map, current + weight * frame_tile, (top_e...  206 us
    another operation x1, loops' own time, track_tiles(): return lax.fori_loop(0, tiles_count, tile_step, start)  131 us
    reduce_sum x64, other arithmetic, tile_step(): score_value = jnp.sum(frame_tile * window) / TS  102 us
    add x64, other arithmetic, tile_step(): current + weight * frame_tile  65 us
    all_to_all x1, waiting for transfers between devices, per_device(): lax.all_to_all(calibrated, 'mod', split_axis=1, concat_axis=2, tiled=True)  47.6 us
  transfers between devices with their start and end apart: 3, of which 2 were waited for; matrix products, arithmetic and copies ran while one was open for 1% of the time, Pallas kernels for 0%

commit v1 on v0

--- a/solution.py
+++ b/solution.py
@@ -78,7 +78,15 @@
     weights = jax.nn.sigmoid(scores)
     all_weights, all_rows, all_cols = (
         lax.all_gather(weights, ("mod", "pulse"), axis=0, tiled=True),
-        lax.all_gather(shift_rows.astype(jnp.float32), ("mod", "pulse"), axis=0, tiled=True),
+        jnp.concatenate(
+            lax.all_to_all(
+                jnp.stack([shift_rows.astype(jnp.float32)] * lax.axis_size(("mod", "pulse"))),
+                ("mod", "pulse"),
+                0,
+                0,
+            ),
+            axis=0,
+        ),
         lax.all_gather(shift_cols.astype(jnp.float32), ("mod", "pulse"), axis=0, tiled=True),
     )
     tiles_across = width // TS

time: 1830 us -> 1510 us (0.83)
  blocking collectives: 683 us -> 348 us
    all_gather x1 -> x0, blocking collectives: 343 us -> none  [recount(): lax.all_gather(shift_rows.astype(jnp.float32), ('mod', 'pulse'), axis=0,...]
  transfers between devices with their start and end apart: 3 -> 4, of which waited for: 2 -> 2; matrix products, arithmetic and copies ran while one was open for 1% -> 1% of each run, Pallas kernels for 0% -> 0%
where the time goes in v1:
time: 1510 us; the launch traced here: 1490 us
  waiting for transfers between devices  409 us (27%)
  blocking collectives  348 us (23%)
  local copies, waits for them, and re-layouts  308 us (20%)
  other arithmetic  228 us (15%)
  loops' own time  132 us (9%)
  matrix products  32.6 us (2%)
  starting transfers between devices  22.8 us (2%)
    all_gather x1, waiting for transfers between devices, per_device(): lax.all_gather(reference_image, ('mod', 'pulse'), axis=0, tiled=True)  361 us
    all_gather x1, blocking collectives, recount(): lax.all_gather(shift_cols.astype(jnp.float32), ('mod', 'pulse'), axis=0,...  348 us
    dynamic_update_slice x64, local copies, waits for them, and re-layouts, tile_step(): lax.dynamic_update_slice(splat_map, current + weight * frame_tile, (top_e...  205 us
    another operation x1, loops' own time, track_tiles(): return lax.fori_loop(0, tiles_count, tile_step, start)  131 us
    reduce_sum x64, other arithmetic, tile_step(): score_value = jnp.sum(frame_tile * window) / TS  102 us
    add x64, other arithmetic, tile_step(): current + weight * frame_tile  65 us
    all_to_all x1, waiting for transfers between devices, per_device(): lax.all_to_all(calibrated, 'mod', split_axis=1, concat_axis=2, tiled=True)  47.6 us
    convert_element_type x1, other arithmetic, calibrate(): ((raw_frames.astype(jnp.float32) - dark_level) * factor).astype(jnp.bfloa...  46.8 us
  transfers between devices with their start and end apart: 4, of which 2 were waited for; matrix products, arithmetic and copies ran while one was open for 1% of the time, Pallas kernels for 0%

profile of v1, /device:TPU:1, one launch (start us, length us, event | category | flops | bytes accessed | tf_op | source)
XLA Modules:
  0.0 1494.9 jit_solution(4668315285427713560)
XLA Ops:
  11.3 46.8 %multiply_convert_fusion = bf16[1,16,1,128,512]{4,3,2,0,1:T(8,128)(2,1)} fusion(bf16[1,16,1,128,512]{4,3,2,1,0:T(8,128)(2,1)S(1)} %copy-done.1, f32[128,512]{1,0:T(8,128)S(1)} %get-tuple-element.391, f32[128,512]{1,0:T(8,128)S(1)} %get-tuple-element.392, f32[128,512]{1,0:T(8,128)S(1)} %get-tuple-element.390, f32[128,512]{1,0:T(8,128)S(1)} %get-tuple-element.398, ...), kind=kLoop, calls=%fused_computation.36 | loop fusion | flops 23068672 | bytes 6423040 | tf_op jit(solution)/shard_map/convert_element_type | solution.py:29
  58.2 10.2 all-to-all-start
  69.3 47.6 %all-to-all-done = bf16[1,16,1,128,512]{4,3,2,0,1:T(8,128)(2,1)} async-done(((bf16[1,16,1,128,512]{4,3,2,0,1:T(8,128)(2,1)}), bf16[1,16,1,128,512]{4,3,2,0,1:T(8,128)(2,1)}, u32[]{:S(2)}, u32[]{:S(2)}) %all-to-all-start) | async-done | bytes 2097184 | tf_op jit(solution)/shard_map/all_to_all | solution.py:133
  117.0 3.8 copy.13
  122.6 8.2 fusion.26
  130.8 360.6 %all-gather.5.cloned.1.call-done = bf16[256,4,1024]{2,1,0:T(4,128)(2,1)} async-done(((bf16[1,4,1024]{2,1,0:T(4,128)(2,1)}), bf16[256,4,1024]{2,1,0:T(4,128)(2,1)}) %all-gather.5.cloned.1.call-update) | async-done | bytes 2097168 | tf_op jit(solution)/shard_map/all_gather | solution.py:134
  491.5 3.9 reshape.340
  495.4 4.2 pad.8
  502.2 589.0 %while.40 = (s32[]{:T(128)}, f32[1072,1072]{1,0:T(8,128)}, f32[64]{0:T(128)S(1)}, s32[64]{0:T(128)S(1)}, s32[64]{0:T(128)S(1)}, /*index=5*/bf16[1024,1024]{1,0:T...) while((s32[]{:T(128)}, f32[1072,1072]{1,0:T(8,128)}, ...), condition=%wide.region_2.3_spmd, body=%wide.region_0.2_spmd.sunk | while | flops 114727 | bytes 361614 | solution.py:70
  508.0 3.2 dynamic_update_slice.15
  563.2 3.3 dynamic_update_slice.15
  581.7 3.3 dynamic_update_slice.15
  646.2 3.3 dynamic_update_slice.15
  664.7 3.3 dynamic_update_slice.15
  673.9 3.2 dynamic_update_slice.15
  720.0 3.2 dynamic_update_slice.15
  729.3 3.3 dynamic_update_slice.15
  738.5 3.3 dynamic_update_slice.15
  747.8 3.3 dynamic_update_slice.15
  757.0 3.3 dynamic_update_slice.15
  803.1 3.3 dynamic_update_slice.15
  812.3 3.3 dynamic_update_slice.15
  821.6 3.3 dynamic_update_slice.15
  867.7 3.2 dynamic_update_slice.15
  932.3 3.3 dynamic_update_slice.15
  950.8 3.2 dynamic_update_slice.15
  969.2 3.2 dynamic_update_slice.15
  987.7 3.2 dynamic_update_slice.15
  1091.2 5.5 slice.52
  1098.2 12.4 all-to-all-start.1
  1110.7 348.3 %all-gather.1 = f32[256,1,1,64]{3,2,1,0:T(1,128)S(1)} all-gather(f32[1,1,1,64]{3,2,1,0:T(1,128)S(1)} %get-tuple-element.393), channel_id=3, replica_groups=mesh['mod'=16,'pulse'=16] {'mod','pulse'}, dimensions={0}, use_global_device_ids=true | all-gather | bytes 65792 | tf_op jit(solution)/shard_map/all_gather | solution.py:90
  1461.6 25.1 %while.41 = (s32[]{:T(128)}, f32[4,1024]{1,0:T(4,128)S(1)}, f32[8,2048]{1,0:T(8,128)S(1)}, f32[8,2048]{1,0:T(8,128)S(1)}, f32[8,2048]{1,0:T(8,128)S(1)}, /*index=5*/s32[]{:T(128)}, s32[]{:T(128)}, s32[]{:T(128)}) while((s32[]{:T(128)}, f32[4,1024]{1,0:T(4,128)S(1)}, f32[8,2048]{1,0:T(8,128)S(1)}, ...), condition=%wide.region_5.6_spmd.clone.clone, body=%wide.region_4.5_spmd.clone.clone.sunk | while | flops 107000840 | bytes 155787 | solution.py:126
  (455 shorter events, 435.6 us)
Async XLA Ops:
  7.2 115.4 %copy-start = (bf16[1024,1024]{1,0:T(8,128)(2,1)S(1)}, bf16[1024,1024]{1,0:T(8,128)(2,1)}, u32[]{:S(2)}) copy-start(bf16[1024,1024]{1,0:T(8,128)(2,1)} %param.20) | copy-start | bytes 6291460
  9.3 2.1 copy-start.1
  11.3 58.0 %copy-start.5 = (s32[2,1,1,64]{3,2,1,0:T(1,128)S(1)}, s32[2,1,1,64]{3,2,1,0:T(1,128)}, u32[]{:S(2)}) copy-start(s32[2,1,1,64]{3,2,1,0:T(1,128)} %param.22) | copy-start | bytes 1540
  58.2 58.8 %all-to-all-start = ((bf16[1,16,1,128,512]{4,3,2,0,1:T(8,128)(2,1)}), bf16[1,16,1,128,512]{4,3,2,0,1:T(8,128)(2,1)}, u32[]{:S(2)}, u32[]{:S(2)}) async-start(bf16[1,16,1,128,512]{4,3,2,0,1:T(8,128)(2,1)} %multiply_convert_fusion), calls=%async_computation | async-start | bytes 4194304 | tf_op jit(solution)/shard_map/all_to_all | solution.py:133
  68.3 423.1 %all-gather.5.cloned.1.call-start = ((), (), s32[]{:S(2)}) async-start(), calls=%async_computation.2 | async-start | bytes 2105344 | tf_op jit(solution)/shard_map/all_gather | solution.py:134
  69.1 1391.6 %all-reduce.6.cloned.1.call-start = ((), (), s32[]{:S(2)}) async-start(), calls=%async_computation.3 | async-start | bytes 8519680
  1091.2 5.5 copy-start.4
  1096.8 0.6 copy-start.2
  1098.2 361.0 %all-to-all-start.1 = ((f32[256,1,64]{2,1,0:T(1,128)}), f32[256,1,64]{2,1,0:T(1,128)S(1)}, u32[]{:S(2)}, u32[]{:S(2)}) async-start(f32[256,1,64]{2,1,0:T(1,128)} %stack.2), calls=%async_computation.1 | async-start | bytes 262144 | tf_op jit(solution)/shard_map/all_to_all | solution.py:82
  1461.5 25.2 %copy-start.3 = (bf16[4,1024]{1,0:T(4,128)(2,1)S(1)}, bf16[4,1024]{1,0:T(4,128)(2,1)}, u32[]{:S(2)}) copy-start(bf16[4,1024]{1,0:T(4,128)(2,1)} %param.21) | copy-start | bytes 24580
Sparse Core Ops, SparseCore 0:
  71.0 420.3 all-gather.4
  1097.6 271.5 all-reduce.5
